TPU v7x, 32 devices: a whole 2x2x4 slice. The times are simulated.
32 devices in a mesh: expert: 8 (over z, core), tensor: 4 (over y, x).
Axes of the slice: x: 2, y: 2, z: 4, core: 2. Of those that a mesh axis runs over, the one named last changes fastest.
Arguments:
- tokens: bfloat16 [256, 4096], P('expert', 'tensor'), may hold values from -6 to 6
- cotangent: bfloat16 [256, 4096], P('expert', 'tensor'), may hold values from -6 to 6
- expert_ids: int32 [256, 8], P('expert'), may hold values from 0 to 63, all different within a row; in each aligned block of 32 rows (0 to 31, 32 to 63, ...) at most 8 rows name the same one
- route_weight: float32 [256, 8], P('expert'), may hold values from 0.05 to 0.25
- w_gate: bfloat16 [64, 4096, 1536], P('expert', 'tensor'), may hold values from -0.09375 to 0.09375
- w_up: bfloat16 [64, 4096, 1536], P('expert', 'tensor'), may hold values from -0.09375 to 0.09375
- w_down: bfloat16 [64, 1536, 4096], P('expert', None, 'tensor'), may hold values from -0.15625 to 0.15625
Outputs:
- mixed_out: bfloat16 [256, 4096], P('expert', 'tensor')
- input_grad: bfloat16 [256, 4096], P('expert', 'tensor')
- down_grad: bfloat16 [64, 1536, 4096], P('expert', None, 'tensor')
Inputs may be any that keep to these rules, and one draw needn't show every extreme that they name: `expert_ids`: each row names 8 different experts; within the 32 rows of one device no expert is named more than 8 times.
All inputs are finite; a program needn't handle non-finite values.
Results may differ from a plain program's by a relative error of at most 0.023.
Values may be sent and summed in bfloat16 or wider, within the bound.
No kernel may reach another device: no remote copies, remote signals or barrier semaphores. Data moves between devices by JAX's collectives and lax.ppermute only.
A program may use at most 192 MiB of HBM per device.

v0:
```python
import jax
import jax.numpy as jnp
from jax import lax
from jax.sharding import PartitionSpec as P


def local(tokens, cotangent, expert_ids, route_weight, w_gate, w_up, w_down):
    resident_specialists = w_gate.shape[0]
    experts = resident_specialists * lax.axis_size("expert")
    tok_count = expert_ids.shape[0]
    top_count = expert_ids.shape[1]
    capacity = 2 * tok_count * top_count // experts
    model_width = tokens.shape[1]
    flat_ids = expert_ids.reshape(-1)
    onehot = (flat_ids[:, None] == jnp.arange(experts, dtype=jnp.int32)[None, :]).astype(jnp.int32)
    before = jnp.cumsum(onehot, axis=0) - onehot
    slot_index = jnp.sum(before * onehot, axis=1)
    target = flat_ids * capacity + slot_index
    chosen = (target[:, None] == jnp.arange(experts * capacity, dtype=jnp.int32)[None, :]).astype(
        jnp.float32
    )
    chosen = chosen.reshape(tok_count, top_count, experts * capacity)
    expert_assignment = jnp.sum(chosen, axis=1)
    weighted = jnp.sum(chosen * route_weight[:, :, None], axis=1)
    token_send = jnp.dot(
        expert_assignment.T.astype(jnp.bfloat16), tokens, preferred_element_type=jnp.float32
    )
    token_send = token_send.astype(jnp.bfloat16).reshape(experts, capacity, model_width)
    gradient_outgoing = jnp.dot(
        weighted.T, cotangent, precision=lax.Precision.HIGHEST, preferred_element_type=jnp.float32
    )
    gradient_outgoing = gradient_outgoing.astype(jnp.bfloat16).reshape(
        experts, capacity, model_width
    )
    token_rows, grad_rows = (
        lax.all_to_all(token_send, "expert", split_axis=0, concat_axis=1, tiled=True),
        lax.all_to_all(gradient_outgoing, "expert", split_axis=0, concat_axis=1, tiled=True),
    )
    pre_gate = jnp.einsum("erd,edf->erf", token_rows, w_gate, preferred_element_type=jnp.float32)
    pre_up = jnp.einsum("erd,edf->erf", token_rows, w_up, preferred_element_type=jnp.float32)
    slice_breadth = w_gate.shape[2] // lax.axis_size("tensor")
    gate_sum, up_sum = (
        lax.psum(pre_gate.astype(jnp.bfloat16), "tensor").astype(jnp.float32),
        lax.psum(pre_up.astype(jnp.bfloat16), "tensor").astype(jnp.float32),
    )
    sigmoid_all = jax.nn.sigmoid(gate_sum)
    hidden = (gate_sum * sigmoid_all * up_sum).astype(jnp.bfloat16)
    out_rows = jnp.einsum(
        "erf,efd->erd", hidden, w_down, preferred_element_type=jnp.float32
    ).astype(jnp.bfloat16)
    down_grad = jnp.einsum("erf,erd->efd", hidden, grad_rows, preferred_element_type=jnp.float32)
    offset = lax.axis_index("tensor") * slice_breadth
    gate_part = lax.dynamic_slice_in_dim(gate_sum, offset, slice_breadth, 2)
    up_part = lax.dynamic_slice_in_dim(up_sum, offset, slice_breadth, 2)
    sigmoid_part = lax.dynamic_slice_in_dim(sigmoid_all, offset, slice_breadth, 2)
    hidden_term = jnp.einsum("erd,efd->erf", grad_rows, w_down, preferred_element_type=jnp.float32)
    hidden_grad = lax.psum_scatter(
        hidden_term.astype(jnp.bfloat16), "tensor", scatter_dimension=2, tiled=True
    ).astype(jnp.float32)
    gate_grad = (
        hidden_grad * up_part * sigmoid_part * (1.0 + gate_part * (1.0 - sigmoid_part))
    ).astype(jnp.bfloat16)
    up_grad = (hidden_grad * gate_part * sigmoid_part).astype(jnp.bfloat16)
    gate_piece = lax.all_gather(gate_grad, "tensor", axis=2, tiled=True)
    up_piece = lax.all_gather(up_grad, "tensor", axis=2, tiled=True)
    running = jnp.einsum("erf,edf->erd", gate_piece, w_gate, preferred_element_type=jnp.float32)
    input_rows = running + jnp.einsum(
        "erf,edf->erd", up_piece, w_up, preferred_element_type=jnp.float32
    )
    input_rows = input_rows.astype(jnp.bfloat16)
    returned_out, returned_in = (
        lax.all_to_all(out_rows, "expert", split_axis=1, concat_axis=0, tiled=True),
        lax.all_to_all(input_rows, "expert", split_axis=1, concat_axis=0, tiled=True),
    )
    returned_out = returned_out.reshape(experts * capacity, model_width)
    returned_in = returned_in.reshape(experts * capacity, model_width)
    mixed_out = jnp.dot(
        weighted, returned_out, precision=lax.Precision.HIGHEST, preferred_element_type=jnp.float32
    )
    input_grad = jnp.dot(
        expert_assignment.astype(jnp.bfloat16), returned_in, preferred_element_type=jnp.float32
    )
    return (
        mixed_out.astype(jnp.bfloat16),
        input_grad.astype(jnp.bfloat16),
        down_grad.astype(jnp.bfloat16),
    )


def solution(mesh):
    return jax.shard_map(
        local,
        mesh=mesh,
        in_specs=(
            P("expert", "tensor"),
            P("expert", "tensor"),
            P("expert", None),
            P("expert", None),
            P("expert", "tensor", None),
            P("expert", "tensor", None),
            P("expert", None, "tensor"),
        ),
        out_specs=(P("expert", "tensor"), P("expert", "tensor"), P("expert", None, "tensor")),
        check_vma=False,
    )
```

profile of v0, /device:TPU:0, one launch (start us, length us, event | category | flops | bytes accessed | tf_op | source)
XLA Modules:
  0.0 326.9 jit_solution(5938493697258200641)
XLA Ops:
  11.0 1.4 fusion
  12.4 6.4 %all-to-all-start = ((bf16[64,8,1024]{2,1,0:T(8,128)(2,1)}), bf16[64,8,1024]{2,1,0:T(8,128)(2,1)S(1)}, u32[]{:S(2)}, u32[]{:S(2)}) async-start(bf16[64,8,1024]{2,1,0:T(8,128)(2,1)} %fusion), calls=%async_computation | async-start | bytes 2097152 | tf_op jit(solution)/shard_map/all_to_all | solution.py:36
  18.8 2.0 fusion.1
  20.8 24.5 %all-to-all-done = bf16[64,8,1024]{2,1,0:T(8,128)(2,1)S(1)} async-done(((bf16[64,8,1024]{2,1,0:T(8,128)(2,1)}), bf16[64,8,1024]{2,1,0:T(8,128)(2,1)S(1)}, u32[]{:S(2)}, u32[]{:S(2)}) %all-to-all-start) | async-done | bytes 1048608 | tf_op jit(solution)/shard_map/all_to_all | solution.py:36
  45.4 3.6 %all-to-all-start.2 = ((bf16[64,8,1024]{2,1,0:T(8,128)(2,1)}), bf16[64,8,1024]{2,1,0:T(8,128)(2,1)S(1)}, u32[]{:S(2)}, u32[]{:S(2)}) async-start(bf16[64,8,1024]{2,1,0:T(8,128)(2,1)} %fusion.1), calls=%async_computation.2 | async-start | bytes 2097152 | tf_op jit(solution)/shard_map/all_to_all | solution.py:37
  49.0 13.7 %convolution_convert_fusion.2 = bf16[8,64,1536]{2,1,0:T(8,128)(2,1)} fusion(bf16[8,1024,1536]{2,1,0:T(8,128)(2,1)} %param.12, bf16[8,8,8,1024]{3,2,1,0:T(8,128)(2,1)S(1)} %bitcast.68), kind=kOutput, calls=%fused_computation.4 | convolution fusion | flops 1611399168 | bytes 27787264 | tf_op jit(solution)/shard_map/erd,edf->erf/dot_general | solution.py:40
  62.7 13.7 %convolution_convert_fusion.3 = bf16[8,64,1536]{2,1,0:T(8,128)(2,1)} fusion(bf16[8,1024,1536]{2,1,0:T(8,128)(2,1)} %param.11, bf16[8,8,8,1024]{3,2,1,0:T(8,128)(2,1)S(1)} %bitcast.69), kind=kOutput, calls=%fused_computation.5 | convolution fusion | flops 1611399168 | bytes 27787264 | tf_op jit(solution)/shard_map/erd,edf->erf/dot_general | solution.py:39
  76.5 13.2 %convolution_convert_fusion.1 = bf16[8,64,1536]{2,1,0:T(8,128)(2,1)S(1)} fusion(bf16[8,1536,1024]{2,1,0:T(8,128)(2,1)} %param.13, bf16[8,8,8,1024]{3,2,1,0:T(8,128)(2,1)S(1)} %bitcast.65), kind=kOutput, calls=%fused_computation.3 | convolution fusion | flops 1611399168 | bytes 27787264 | tf_op jit(solution)/shard_map/erd,efd->erf/dot_general | solution.py:56
  89.7 3.5 %copy.60 = bf16[8,64,1536]{1,0,2:T(8,128)(2,1)} copy(bf16[8,64,1536]{2,1,0:T(8,128)(2,1)S(1)} %convolution_convert_fusion.1) | data formatting | bytes 3145728
  93.2 5.4 %reshape.61 = bf16[1536,512]{1,0:T(8,128)(2,1)} reshape(bf16[1536,8,64]{2,1,0:T(8,128)(2,1)} %bitcast.67) | data formatting | bytes 3145728
  98.9 66.0 %all-reduce.3.cloned.1.call-done = (bf16[8,64,1536]{2,1,0:T(8,128)(2,1)}, bf16[8,64,1536]{2,1,0:T(8,128)(2,1)}) async-done(((bf16[8,64,1536]{2,1,0:T(8,128)(2,1)}, bf16[8,64,1536]{2,1,0:T(8,128)(2,1)}), (bf16[8,64,1536]{2,1,0:T(8,128)(2,1)}, bf16[8,64,1536]{2,1,0:T(8,128)(2,1)})) %all-reduce.3.cloned.1.call-update) | async-done | bytes 3145744 | tf_op jit(solution)/shard_map/psum | solution.py:43
  164.9 3.6 %convert_element_type.70 = f32[8,64,1536]{2,1,0:T(8,128)} convert(bf16[8,64,1536]{2,1,0:T(8,128)(2,1)} %get-tuple-element.5) | non-fusion elementwise | flops 786432 | bytes 4718592 | tf_op jit(solution)/shard_map/convert_element_type | solution.py:43
  168.5 2.5 add_divide_fusion
  171.0 28.1 %reduce-scatter.4.cloned.1.call-done = bf16[384,512]{1,0:T(8,128)(2,1)} async-done(((bf16[1536,512]{1,0:T(8,128)(2,1)}), bf16[384,512]{1,0:T(8,128)(2,1)}) %reduce-scatter.4.cloned.1.call-update) | async-done | bytes 393232
  199.0 1.5 reshape.62
  200.6 1.3 copy.61
  201.8 1.8 convert_element_type.72
  203.7 2.6 fusion.14
  206.9 13.5 %convolution_convert_fusion.4 = bf16[8,64,1024]{2,1,0:T(8,128)(2,1)S(1)} fusion(bf16[8,1536,1024]{2,1,0:T(8,128)(2,1)} %param.13, bf16[8,64,1536]{2,1,0:T(8,128)(2,1)S(1)} %copy-done.2, bf16[8,64,1536]{2,1,0:T(8,128)(2,1)} %get-tuple-element.6), kind=kOutput, calls=%fused_computation.7 | convolution fusion | flops 1617428480 | bytes 29360128 | tf_op jit(solution)/shard_map/erf,efd->erd/dot_general | solution.py:48
  220.4 1.6 copy.51
  222.0 4.6 %all-to-all-start.1 = ((bf16[8,64,1024]{2,0,1:T(8,128)(2,1)}), bf16[8,64,1024]{2,0,1:T(8,128)(2,1)}, u32[]{:S(2)}, u32[]{:S(2)}) async-start(bf16[8,64,1024]{2,0,1:T(8,128)(2,1)} %copy.51), calls=%async_computation.1 | async-start | bytes 2097152 | tf_op jit(solution)/shard_map/all_to_all | solution.py:72
  226.6 10.6 %all-gather.3.cloned.1.call-done = bf16[8,64,1536]{2,1,0:T(8,128)(2,1)} async-done(((bf16[8,64,384]{2,1,0:T(8,128)(2,1)}), bf16[8,64,1536]{2,1,0:T(8,128)(2,1)}) %all-gather.3.cloned.1.call-update) | async-done | bytes 1572880 | tf_op jit(solution)/shard_map/all_gather | solution.py:64
  237.2 13.8 %fusion.21 = f32[8,64,1024]{2,1,0:T(8,128)} fusion(bf16[8,64,1536]{2,1,0:T(8,128)(2,1)} %all-gather.3.cloned.1.call-done, bf16[8,1024,1536]{2,1,0:T(8,128)(2,1)} %param.11), kind=kOutput, calls=%fused_computation.44 | convolution fusion | flops 1610612736 | bytes 28835840 | tf_op jit(solution)/shard_map/erf,edf->erd/dot_general | solution.py:66
  251.0 18.6 %all-gather.5.cloned.1.call-done = bf16[8,64,1536]{2,1,0:T(8,128)(2,1)} async-done(((bf16[8,64,384]{2,1,0:T(8,128)(2,1)}), bf16[8,64,1536]{2,1,0:T(8,128)(2,1)}) %all-gather.5.cloned.1.call-update) | async-done | bytes 1572880 | tf_op jit(solution)/shard_map/all_gather | solution.py:65
  269.6 14.0 %add_convert_fusion = bf16[8,64,1024]{2,1,0:T(8,128)(2,1)} fusion(f32[8,64,1024]{2,1,0:T(8,128)} %fusion.21, bf16[8,64,1536]{2,1,0:T(8,128)(2,1)} %all-gather.5.cloned.1.call-done, bf16[8,1024,1536]{2,1,0:T(8,128)(2,1)} %param.12), kind=kOutput, calls=%fused_computation.6 | convolution fusion | flops 1611661312 | bytes 29884416 | tf_op jit(solution)/shard_map/erf,edf->erd/dot_general | solution.py:67
  283.6 2.8 copy.55
  286.3 4.6 %all-to-all-start.3 = ((bf16[8,64,1024]{2,0,1:T(8,128)(2,1)}), bf16[8,64,1024]{2,0,1:T(8,128)(2,1)}, u32[]{:S(2)}, u32[]{:S(2)}) async-start(bf16[8,64,1024]{2,0,1:T(8,128)(2,1)} %copy.55), calls=%async_computation.3 | async-start | bytes 2097152 | tf_op jit(solution)/shard_map/all_to_all | solution.py:73
  291.0 13.8 %convolution_convert_fusion = bf16[8,1536,1024]{2,1,0:T(8,128)(2,1)} fusion(bf16[8,8,8,1024]{3,2,1,0:T(8,128)(2,1)S(1)} %bitcast.66, bf16[8,64,1536]{2,1,0:T(8,128)(2,1)S(1)} %copy-done.2, bf16[8,64,1536]{2,1,0:T(8,128)(2,1)} %get-tuple-element.6), kind=kOutput, calls=%fused_computation | convolution fusion | flops 1629487104 | bytes 29360128 | tf_op jit(solution)/shard_map/erf,erd->efd/dot_general | solution.py:51
  304.8 1.9 copy.53
  306.6 1.2 convolution_convert_fusion.8
  307.9 9.8 %all-to-all-done.3 = bf16[8,64,1024]{2,0,1:T(8,128)(2,1)} async-done(((bf16[8,64,1024]{2,0,1:T(8,128)(2,1)}), bf16[8,64,1024]{2,0,1:T(8,128)(2,1)}, u32[]{:S(2)}, u32[]{:S(2)}) %all-to-all-start.3) | async-done | bytes 1048608 | tf_op jit(solution)/shard_map/all_to_all | solution.py:73
  317.6 1.8 copy.57
  (38 shorter events, 5.7 us)
Async XLA Ops:
  7.2 3.9 %copy-start = (bf16[32,1024]{1,0:T(8,128)(2,1)S(1)}, bf16[32,1024]{1,0:T(8,128)(2,1)}, u32[]{:S(2)}) copy-start(bf16[32,1024]{1,0:T(8,128)(2,1)} %param.7) | copy-start | bytes 196612
  7.2 11.6 %copy-start.6 = (bf16[32,1024]{1,0:T(8,128)(2,1)S(1)}, bf16[32,1024]{1,0:T(8,128)(2,1)}, u32[]{:S(2)}) copy-start(bf16[32,1024]{1,0:T(8,128)(2,1)} %param.8) | copy-start | bytes 196612
  10.4 0.6 copy-start.4
  12.4 32.9 %all-to-all-start = ((bf16[64,8,1024]{2,1,0:T(8,128)(2,1)}), bf16[64,8,1024]{2,1,0:T(8,128)(2,1)S(1)}, u32[]{:S(2)}, u32[]{:S(2)}) async-start(bf16[64,8,1024]{2,1,0:T(8,128)(2,1)} %fusion), calls=%async_computation | async-start | bytes 2097152 | tf_op jit(solution)/shard_map/all_to_all | solution.py:36
  45.4 31.1 %all-to-all-start.2 = ((bf16[64,8,1024]{2,1,0:T(8,128)(2,1)}), bf16[64,8,1024]{2,1,0:T(8,128)(2,1)S(1)}, u32[]{:S(2)}, u32[]{:S(2)}) async-start(bf16[64,8,1024]{2,1,0:T(8,128)(2,1)} %fusion.1), calls=%async_computation.2 | async-start | bytes 2097152 | tf_op jit(solution)/shard_map/all_to_all | solution.py:37
  48.9 116.0 %all-reduce.3.cloned.1.call-start = ((), (), s32[]{:S(2)}) async-start(), calls=%async_computation.8 | async-start | bytes 6291456 | tf_op jit(solution)/shard_map/psum | solution.py:43
  76.4 122.6 %reduce-scatter.4.cloned.1.call-start = ((), (), s32[]{:S(2)}) async-start(), calls=%async_computation.7 | async-start | bytes 1966080
  98.6 138.5 %all-gather.3.cloned.1.call-start = ((), (), s32[]{:S(2)}) async-start(), calls=%async_computation.5 | async-start | bytes 1966080 | tf_op jit(solution)/shard_map/all_gather | solution.py:64
  164.9 3.6 %copy-start.2 = (bf16[8,64,1536]{2,1,0:T(8,128)(2,1)S(1)}, bf16[8,64,1536]{2,1,0:T(8,128)(2,1)}, u32[]{:S(2)}) copy-start(bf16[8,64,1536]{2,1,0:T(8,128)(2,1)} %get-tuple-element.5) | copy-start | bytes 4718596
  201.8 1.9 copy-start.3
  206.3 63.3 %all-gather.5.cloned.1.call-start = ((), (), s32[]{:S(2)}) async-start(), calls=%async_computation.6 | async-start | bytes 1966080 | tf_op jit(solution)/shard_map/all_gather | solution.py:65
  222.0 64.3 %all-to-all-start.1 = ((bf16[8,64,1024]{2,0,1:T(8,128)(2,1)}), bf16[8,64,1024]{2,0,1:T(8,128)(2,1)}, u32[]{:S(2)}, u32[]{:S(2)}) async-start(bf16[8,64,1024]{2,0,1:T(8,128)(2,1)} %copy.51), calls=%async_computation.1 | async-start | bytes 2097152 | tf_op jit(solution)/shard_map/all_to_all | solution.py:72
  286.3 31.3 %all-to-all-start.3 = ((bf16[8,64,1024]{2,0,1:T(8,128)(2,1)}), bf16[8,64,1024]{2,0,1:T(8,128)(2,1)}, u32[]{:S(2)}, u32[]{:S(2)}) async-start(bf16[8,64,1024]{2,0,1:T(8,128)(2,1)} %copy.55), calls=%async_computation.3 | async-start | bytes 2097152 | tf_op jit(solution)/shard_map/all_to_all | solution.py:73
  304.8 14.7 %copy-start.5 = (bf16[32,512]{1,0:T(8,128)(2,1)S(1)}, bf16[32,512]{1,0:T(8,128)(2,1)}, u32[]{:S(2)}) copy-start(bf16[32,512]{1,0:T(8,128)(2,1)} %copy-done.4) | copy-start | bytes 98308
  304.8 15.6 %copy-start.1 = (bf16[32,1024]{1,0:T(8,128)(2,1)S(1)}, bf16[32,1024]{1,0:T(8,128)(2,1)}, u32[]{:S(2)}) copy-start(bf16[32,1024]{1,0:T(8,128)(2,1)} %param.7) | copy-start | bytes 196612
Sparse Core Ops, SparseCore 0:
  76.5 88.3 all-reduce.2
  167.9 31.1 reduce-scatter.3
  206.4 30.6 all-gather.2
  238.8 30.6 all-gather.4
where the time goes:
time: 328 us; the launch traced here: 327 us
  waiting for transfers between devices  158 us (48%)
  matrix products  101 us (31%)
  local copies, waits for them, and re-layouts  22.4 us (7%)
  starting transfers between devices  19.4 us (6%)
  between operations  13.9 us (4%)
  other arithmetic  11.7 us (4%)
    psum x1, waiting for transfers between devices, local(): lax.psum(pre_gate.astype(jnp.bfloat16), 'tensor').astype(jnp.float32)  66 us
    unnamed x5, waiting for transfers between devices  28.6 us
    all_to_all x1, waiting for transfers between devices, local(): lax.all_to_all(token_send, 'expert', split_axis=0, concat_axis=1, tiled=T...  24.5 us
    all_gather x1, waiting for transfers between devices, local(): up_piece = lax.all_gather(up_grad, 'tensor', axis=2, tiled=True)  18.6 us
    dot_general x1, matrix products, local(): jnp.einsum('erf,edf->erd', up_piece, w_up, preferred_element_type=jnp.flo...  14 us
    unnamed x20, local copies, waits for them, and re-layouts  13.9 us
    dot_general x1, matrix products, local(): jnp.einsum('erf,erd->efd', hidden, grad_rows, preferred_element_type=jnp....  13.8 us
    dot_general x1, matrix products, local(): jnp.einsum('erf,edf->erd', gate_piece, w_gate, preferred_element_type=jnp...  13.8 us
  transfers between devices with their start and end apart: 8, of which 6 were waited for; matrix products, arithmetic and copies ran while one was open for 37% of the time, Pallas kernels for 0%

commit v1 on v0

--- a/solution.py
+++ b/solution.py
@@ -2,6 +2,18 @@
 import jax.numpy as jnp
 from jax import lax
 from jax.sharding import PartitionSpec as P
+
+
+def summed_around(value, axis, dim, product):
+    size, index, extent = (lax.axis_size(axis), lax.axis_index(axis), value.shape[dim])
+    upward = [(i, (i + 1) % size) for i in range(size)]
+    block, total = (value, None)
+    for step in range(size):
+        coming = lax.ppermute(block, axis, upward) if step < size - 1 else None
+        absorb = product(block, (index - step) % size * extent)
+        total = absorb if total is None else total + absorb
+        block = coming
+    return total
 
 
 def local(tokens, cotangent, expert_ids, route_weight, w_gate, w_up, w_down):
@@ -62,10 +74,17 @@
     ).astype(jnp.bfloat16)
     up_grad = (hidden_grad * gate_part * sigmoid_part).astype(jnp.bfloat16)
     gate_piece = lax.all_gather(gate_grad, "tensor", axis=2, tiled=True)
-    up_piece = lax.all_gather(up_grad, "tensor", axis=2, tiled=True)
     running = jnp.einsum("erf,edf->erd", gate_piece, w_gate, preferred_element_type=jnp.float32)
-    input_rows = running + jnp.einsum(
-        "erf,edf->erd", up_piece, w_up, preferred_element_type=jnp.float32
+    input_rows = running + summed_around(
+        up_grad,
+        "tensor",
+        2,
+        lambda own_block, start: jnp.einsum(
+            "erf,edf->erd",
+            own_block,
+            lax.dynamic_slice_in_dim(w_up, start, own_block.shape[2], axis=2),
+            preferred_element_type=jnp.float32,
+        ),
     )
     input_rows = input_rows.astype(jnp.bfloat16)
     returned_out, returned_in = (

time: 328 us -> 317 us (0.966)
  waiting for transfers between devices: 158 us -> 134 us
  matrix products: 101 us -> 113 us
    all_gather x1 -> x0, waiting for transfers between devices: 18.6 us -> none  [local(): up_piece = lax.all_gather(up_grad, 'tensor', axis=2, tiled=True)]
    dot_general x1 -> x4, matrix products: 14 us -> 26.1 us  [local(): jnp.einsum('erf,edf->erd', own_block, lax.dynamic_slice_in_dim(w_up, star...]
    all_gather x1, waiting for transfers between devices: 10.6 us -> 0.01 us  [local(): gate_piece = lax.all_gather(gate_grad, 'tensor', axis=2, tiled=True)]
    ppermute x0 -> x3, waiting for transfers between devices: none -> 5.86 us  [summed_around(): coming = lax.ppermute(block, axis, upward) if step < size - 1 else None]
    unnamed x20 -> x16, local copies, waits for them, and re-layouts: 13.9 us -> 13.2 us
    unnamed x5 -> x4, waiting for transfers between devices: 28.6 us -> 28.1 us
  transfers between devices with their start and end apart: 8 -> 10, of which waited for: 6 -> 5; matrix products, arithmetic and copies ran while one was open for 37% -> 41% of each run, Pallas kernels for 0% -> 0%
where the time goes in v1:
time: 317 us; the launch traced here: 316 us
  waiting for transfers between devices  134 us (42%)
  matrix products  113 us (36%)
  starting transfers between devices  22.4 us (7%)
  local copies, waits for them, and re-layouts  20.6 us (6%)
  between operations  14 us (4%)
  other arithmetic  11.6 us (4%)
    psum x1, waiting for transfers between devices, local(): lax.psum(pre_gate.astype(jnp.bfloat16), 'tensor').astype(jnp.float32)  66 us
    unnamed x4, waiting for transfers between devices  28.1 us
    dot_general x4, matrix products, local(): jnp.einsum('erf,edf->erd', own_block, lax.dynamic_slice_in_dim(w_up, star...  26.1 us
    all_to_all x1, waiting for transfers between devices, local(): lax.all_to_all(token_send, 'expert', split_axis=0, concat_axis=1, tiled=T...  24.5 us
    dot_general x1, matrix products, local(): jnp.einsum('erf,erd->efd', hidden, grad_rows, preferred_element_type=jnp....  13.8 us
    dot_general x1, matrix products, local(): jnp.einsum('erf,edf->erd', gate_piece, w_gate, preferred_element_type=jnp...  13.8 us
    dot_general x1, matrix products, local(): jnp.einsum('erd,edf->erf', token_rows, w_up, preferred_element_type=jnp.f...  13.7 us
    dot_general x1, matrix products, local(): jnp.einsum('erd,edf->erf', token_rows, w_gate, preferred_element_type=jnp...  13.7 us
  transfers between devices with their start and end apart: 10, of which 5 were waited for; matrix products, arithmetic and copies ran while one was open for 41% of the time, Pallas kernels for 0%

profile of v1, /device:TPU:0, one launch (start us, length us, event | category | flops | bytes accessed | tf_op | source)
XLA Modules:
  0.0 316.2 jit_solution(13644415257099127169)
XLA Ops:
  11.8 6.4 %all-to-all-start = ((bf16[64,8,1024]{2,1,0:T(8,128)(2,1)}), bf16[64,8,1024]{2,1,0:T(8,128)(2,1)S(1)}, u32[]{:S(2)}, u32[]{:S(2)}) async-start(bf16[64,8,1024]{2,1,0:T(8,128)(2,1)} %fusion.10), calls=%async_computation | async-start | bytes 2097152 | tf_op jit(solution)/shard_map/all_to_all | solution.py:48
  18.2 2.1 fusion.11
  20.3 24.5 %all-to-all-done = bf16[64,8,1024]{2,1,0:T(8,128)(2,1)S(1)} async-done(((bf16[64,8,1024]{2,1,0:T(8,128)(2,1)}), bf16[64,8,1024]{2,1,0:T(8,128)(2,1)S(1)}, u32[]{:S(2)}, u32[]{:S(2)}) %all-to-all-start) | async-done | bytes 1048608 | tf_op jit(solution)/shard_map/all_to_all | solution.py:48
  44.8 3.6 %all-to-all-start.2 = ((bf16[64,8,1024]{2,1,0:T(8,128)(2,1)}), bf16[64,8,1024]{2,1,0:T(8,128)(2,1)S(1)}, u32[]{:S(2)}, u32[]{:S(2)}) async-start(bf16[64,8,1024]{2,1,0:T(8,128)(2,1)} %fusion.11), calls=%async_computation.2 | async-start | bytes 2097152 | tf_op jit(solution)/shard_map/all_to_all | solution.py:49
  48.4 13.7 %convolution_convert_fusion.2 = bf16[8,64,1536]{2,1,0:T(8,128)(2,1)} fusion(bf16[8,1024,1536]{2,1,0:T(8,128)(2,1)} %param.12, bf16[8,8,8,1024]{3,2,1,0:T(8,128)(2,1)S(1)} %bitcast.70), kind=kOutput, calls=%fused_computation.12 | convolution fusion | flops 1611399168 | bytes 27787264 | tf_op jit(solution)/shard_map/erd,edf->erf/dot_general | solution.py:52
  62.1 13.7 %convolution_convert_fusion.3 = bf16[8,64,1536]{2,1,0:T(8,128)(2,1)} fusion(bf16[8,1024,1536]{2,1,0:T(8,128)(2,1)} %param.11, bf16[8,8,8,1024]{3,2,1,0:T(8,128)(2,1)S(1)} %bitcast.71), kind=kOutput, calls=%fused_computation.13 | convolution fusion | flops 1611399168 | bytes 27787264 | tf_op jit(solution)/shard_map/erd,edf->erf/dot_general | solution.py:51
  75.8 13.2 %convolution_convert_fusion.1 = bf16[8,64,1536]{2,1,0:T(8,128)(2,1)S(1)} fusion(bf16[8,1536,1024]{2,1,0:T(8,128)(2,1)} %param.13, bf16[8,8,8,1024]{3,2,1,0:T(8,128)(2,1)S(1)} %bitcast.67), kind=kOutput, calls=%fused_computation.11 | convolution fusion | flops 1611399168 | bytes 27787264 | tf_op jit(solution)/shard_map/erd,efd->erf/dot_general | solution.py:68
  89.1 3.5 %copy.60 = bf16[8,64,1536]{1,0,2:T(8,128)(2,1)} copy(bf16[8,64,1536]{2,1,0:T(8,128)(2,1)S(1)} %convolution_convert_fusion.1) | data formatting | bytes 3145728
  92.5 5.4 %reshape.61 = bf16[1536,512]{1,0:T(8,128)(2,1)} reshape(bf16[1536,8,64]{2,1,0:T(8,128)(2,1)} %bitcast.69) | data formatting | bytes 3145728
  98.3 66.0 %all-reduce.3.cloned.1.call-done = (bf16[8,64,1536]{2,1,0:T(8,128)(2,1)}, bf16[8,64,1536]{2,1,0:T(8,128)(2,1)}) async-done(((bf16[8,64,1536]{2,1,0:T(8,128)(2,1)}, bf16[8,64,1536]{2,1,0:T(8,128)(2,1)}), (bf16[8,64,1536]{2,1,0:T(8,128)(2,1)}, bf16[8,64,1536]{2,1,0:T(8,128)(2,1)})) %all-reduce.3.cloned.1.call-update) | async-done | bytes 3145744 | tf_op jit(solution)/shard_map/psum | solution.py:55
  164.3 3.6 %convert_element_type.70 = f32[8,64,1536]{2,1,0:T(8,128)} convert(bf16[8,64,1536]{2,1,0:T(8,128)(2,1)} %get-tuple-element.5) | non-fusion elementwise | flops 786432 | bytes 4718592 | tf_op jit(solution)/shard_map/convert_element_type | solution.py:55
  167.9 2.5 add_divide_fusion
  170.3 28.1 %reduce-scatter.4.cloned.1.call-done = bf16[384,512]{1,0:T(8,128)(2,1)} async-done(((bf16[1536,512]{1,0:T(8,128)(2,1)}), bf16[384,512]{1,0:T(8,128)(2,1)}) %reduce-scatter.4.cloned.1.call-update) | async-done | bytes 393232
  198.4 1.5 reshape.62
  201.2 1.8 convert_element_type.72
  203.0 2.5 fusion.24
  205.5 1.5 collective-permute-start
  207.0 13.5 %convolution_convert_fusion.4 = bf16[8,64,1024]{2,1,0:T(8,128)(2,1)S(1)} fusion(bf16[8,1536,1024]{2,1,0:T(8,128)(2,1)} %param.13, bf16[8,64,1536]{2,1,0:T(8,128)(2,1)S(1)} %copy-done.2, bf16[8,64,1536]{2,1,0:T(8,128)(2,1)} %get-tuple-element.6), kind=kOutput, calls=%fused_computation.15 | convolution fusion | flops 1617428480 | bytes 29360128 | tf_op jit(solution)/shard_map/erf,efd->erd/dot_general | solution.py:60
  220.6 1.6 copy.51
  222.1 4.6 %all-to-all-start.1 = ((bf16[8,64,1024]{2,0,1:T(8,128)(2,1)}), bf16[8,64,1024]{2,0,1:T(8,128)(2,1)}, u32[]{:S(2)}, u32[]{:S(2)}) async-start(bf16[8,64,1024]{2,0,1:T(8,128)(2,1)} %copy.51), calls=%async_computation.1 | async-start | bytes 2097152 | tf_op jit(solution)/shard_map/all_to_all | solution.py:91
  228.2 6.2 %fusion.6 = f32[8,64,1024]{2,1,0:T(8,128)} fusion(bf16[8,64,384]{2,1,0:T(8,128)(2,1)S(1)} %get-tuple-element.7, bf16[8,1024,1536]{2,1,0:T(8,128)(2,1)} %param.12, s32[]{:T(128)S(6)} %select_n.38), kind=kOutput, calls=%fused_computation.7 | convolution fusion | flops 402653184 | bytes 8781828 | tf_op jit(solution)/shard_map/erf,edf->erd/dot_general | solution.py:82
  234.4 6.3 %fusion.4 = f32[8,64,1024]{2,1,0:T(8,128)} fusion(bf16[8,64,384]{2,1,0:T(8,128)(2,1)} %collective-permute-done, bf16[8,1024,1536]{2,1,0:T(8,128)(2,1)} %param.12, s32[]{:T(128)S(6)} %select_n.40), kind=kOutput, calls=%fused_computation.5 | convolution fusion | flops 402653184 | bytes 8781828 | tf_op jit(solution)/shard_map/erf,edf->erd/dot_general | solution.py:82
  240.8 5.9 %collective-permute-done.1 = bf16[8,64,384]{2,1,0:T(8,128)(2,1)S(1)} collective-permute-done((bf16[8,64,384]{2,1,0:T(8,128)(2,1)}, bf16[8,64,384]{2,1,0:T(8,128)(2,1)S(1)}, u32[]{:S(2)}, u32[]{:S(2)}) %collective-permute-start.1) | collective-permute-done | bytes 393248 | tf_op jit(solution)/shard_map/ppermute | solution.py:12
  246.6 6.2 %fusion.2 = f32[8,64,1024]{2,1,0:T(8,128)} fusion(bf16[8,64,384]{2,1,0:T(8,128)(2,1)S(1)} %collective-permute-done.1, bf16[8,1024,1536]{2,1,0:T(8,128)(2,1)} %param.12, s32[]{:T(128)S(6)} %select_n.42), kind=kOutput, calls=%fused_computation.3 | convolution fusion | flops 402653184 | bytes 8781828 | tf_op jit(solution)/shard_map/erf,edf->erd/dot_general | solution.py:82
  252.8 13.8 %fusion.35 = f32[8,64,1024]{2,1,0:T(8,128)} fusion(bf16[8,64,1536]{2,1,0:T(8,128)(2,1)} %all-gather.2.cloned.1.call-done, bf16[8,1024,1536]{2,1,0:T(8,128)(2,1)} %param.11), kind=kOutput, calls=%fused_computation.56 | convolution fusion | flops 1610612736 | bytes 28835840 | tf_op jit(solution)/shard_map/erf,edf->erd/dot_general | solution.py:77
  266.6 7.4 %add_convert_fusion = bf16[8,64,1024]{2,1,0:T(8,128)(2,1)S(1)} fusion(f32[8,64,1024]{2,1,0:T(8,128)} %fusion.35, f32[8,64,1024]{2,1,0:T(8,128)} %fusion.2, f32[8,64,1024]{2,1,0:T(8,128)} %fusion.6, f32[8,64,1024]{2,1,0:T(8,128)} %fusion.4, bf16[8,64,384]{2,1,0:T(8,128)(2,1)S(1)} %collective-permute-done.2, bf16[8,1024,1536]{2,1,0:T(8,128)(2,1)} %param.12, ...), kind=kOutput, calls=%fused_computation.14 | convolution fusion | flops 405274624 | bytes 16121860 | tf_op jit(solution)/shard_map/erf,edf->erd/dot_general | solution.py:82
  274.0 1.7 copy.55
  275.7 4.6 %all-to-all-start.3 = ((bf16[8,64,1024]{2,0,1:T(8,128)(2,1)}), bf16[8,64,1024]{2,0,1:T(8,128)(2,1)}, u32[]{:S(2)}, u32[]{:S(2)}) async-start(bf16[8,64,1024]{2,0,1:T(8,128)(2,1)} %copy.55), calls=%async_computation.3 | async-start | bytes 2097152 | tf_op jit(solution)/shard_map/all_to_all | solution.py:92
  280.3 13.8 %convolution_convert_fusion = bf16[8,1536,1024]{2,1,0:T(8,128)(2,1)} fusion(bf16[8,8,8,1024]{3,2,1,0:T(8,128)(2,1)S(1)} %bitcast.68, bf16[8,64,1536]{2,1,0:T(8,128)(2,1)S(1)} %copy-done.2, bf16[8,64,1536]{2,1,0:T(8,128)(2,1)} %get-tuple-element.6), kind=kOutput, calls=%fused_computation | convolution fusion | flops 1629487104 | bytes 29360128 | tf_op jit(solution)/shard_map/erf,erd->efd/dot_general | solution.py:63
  294.1 1.9 copy.53
  297.2 9.8 %all-to-all-done.3 = bf16[8,64,1024]{2,0,1:T(8,128)(2,1)} async-done(((bf16[8,64,1024]{2,0,1:T(8,128)(2,1)}), bf16[8,64,1024]{2,0,1:T(8,128)(2,1)}, u32[]{:S(2)}, u32[]{:S(2)}) %all-to-all-start.3) | async-done | bytes 1048608 | tf_op jit(solution)/shard_map/all_to_all | solution.py:92
  306.9 1.8 copy.57
  (40 shorter events, 9.9 us)
Async XLA Ops:
  7.2 3.2 %copy-start = (bf16[32,1024]{1,0:T(8,128)(2,1)S(1)}, bf16[32,1024]{1,0:T(8,128)(2,1)}, u32[]{:S(2)}) copy-start(bf16[32,1024]{1,0:T(8,128)(2,1)} %param.7) | copy-start | bytes 196612
  7.2 11.0 %copy-start.4 = (bf16[32,1024]{1,0:T(8,128)(2,1)S(1)}, bf16[32,1024]{1,0:T(8,128)(2,1)}, u32[]{:S(2)}) copy-start(bf16[32,1024]{1,0:T(8,128)(2,1)} %param.8) | copy-start | bytes 196612
  11.8 32.9 %all-to-all-start = ((bf16[64,8,1024]{2,1,0:T(8,128)(2,1)}), bf16[64,8,1024]{2,1,0:T(8,128)(2,1)S(1)}, u32[]{:S(2)}, u32[]{:S(2)}) async-start(bf16[64,8,1024]{2,1,0:T(8,128)(2,1)} %fusion.10), calls=%async_computation | async-start | bytes 2097152 | tf_op jit(solution)/shard_map/all_to_all | solution.py:48
  44.8 31.1 %all-to-all-start.2 = ((bf16[64,8,1024]{2,1,0:T(8,128)(2,1)}), bf16[64,8,1024]{2,1,0:T(8,128)(2,1)S(1)}, u32[]{:S(2)}, u32[]{:S(2)}) async-start(bf16[64,8,1024]{2,1,0:T(8,128)(2,1)} %fusion.11), calls=%async_computation.2 | async-start | bytes 2097152 | tf_op jit(solution)/shard_map/all_to_all | solution.py:49
  48.3 115.9 %all-reduce.3.cloned.1.call-start = ((), (), s32[]{:S(2)}) async-start(), calls=%async_computation.7 | async-start | bytes 6291456 | tf_op jit(solution)/shard_map/psum | solution.py:55
  75.8 122.6 %reduce-scatter.4.cloned.1.call-start = ((), (), s32[]{:S(2)}) async-start(), calls=%async_computation.6 | async-start | bytes 1966080
  98.0 154.8 %all-gather.2.cloned.1.call-start = ((), (), s32[]{:S(2)}) async-start(), calls=%async_computation.5 | async-start | bytes 1966080 | tf_op jit(solution)/shard_map/all_gather | solution.py:76
  164.3 3.6 %copy-start.2 = (bf16[8,64,1536]{2,1,0:T(8,128)(2,1)S(1)}, bf16[8,64,1536]{2,1,0:T(8,128)(2,1)}, u32[]{:S(2)}) copy-start(bf16[8,64,1536]{2,1,0:T(8,128)(2,1)} %get-tuple-element.5) | copy-start | bytes 4718596
  201.2 1.9 copy-start.3
  205.5 21.2 %collective-permute-start = (bf16[8,64,384]{2,1,0:T(8,128)(2,1)S(1)}, bf16[8,64,384]{2,1,0:T(8,128)(2,1)}, u32[]{:S(2)}, u32[]{:S(2)}) collective-permute-start(bf16[8,64,384]{2,1,0:T(8,128)(2,1)S(1)} %get-tuple-element.7), channel_id=1, source_target_pairs={{0,1},{1,2},{2,3},{3,0},{4,5},{5,6},{6,7},{7,4},{8,9},{9,10},{10,1... | collective-permute-start | bytes 1179656 | tf_op jit(solution)/shard_map/ppermute | solution.py:12
  222.1 53.5 %all-to-all-start.1 = ((bf16[8,64,1024]{2,0,1:T(8,128)(2,1)}), bf16[8,64,1024]{2,0,1:T(8,128)(2,1)}, u32[]{:S(2)}, u32[]{:S(2)}) async-start(bf16[8,64,1024]{2,0,1:T(8,128)(2,1)} %copy.51), calls=%async_computation.1 | async-start | bytes 2097152 | tf_op jit(solution)/shard_map/all_to_all | solution.py:91
  226.7 19.9 %collective-permute-start.1 = (bf16[8,64,384]{2,1,0:T(8,128)(2,1)}, bf16[8,64,384]{2,1,0:T(8,128)(2,1)S(1)}, u32[]{:S(2)}, u32[]{:S(2)}) collective-permute-start(bf16[8,64,384]{2,1,0:T(8,128)(2,1)} %collective-permute-done), channel_id=1, source_target_pairs={{0,1},{1,2},{2,3},{3,0},{4,5},{5,6},{6,7},{7,4},{8,9},{9,10},{10,1... | collective-permute-start | bytes 1179656 | tf_op jit(solution)/shard_map/ppermute | solution.py:12
  246.6 20.0 %collective-permute-start.2 = (bf16[8,64,384]{2,1,0:T(8,128)(2,1)S(1)}, bf16[8,64,384]{2,1,0:T(8,128)(2,1)S(1)}, u32[]{:S(2)}, u32[]{:S(2)}) collective-permute-start(bf16[8,64,384]{2,1,0:T(8,128)(2,1)S(1)} %collective-permute-done.1), channel_id=1, source_target_pairs={{0,1},{1,2},{2,3},{3,0},{4,5},{5,6},{6,7},{7,4},{8,9},{9,10},{10,1... | collective-permute-start | bytes 1179656 | tf_op jit(solution)/shard_map/ppermute | solution.py:12
  275.7 31.3 %all-to-all-start.3 = ((bf16[8,64,1024]{2,0,1:T(8,128)(2,1)}), bf16[8,64,1024]{2,0,1:T(8,128)(2,1)}, u32[]{:S(2)}, u32[]{:S(2)}) async-start(bf16[8,64,1024]{2,0,1:T(8,128)(2,1)} %copy.55), calls=%async_computation.3 | async-start | bytes 2097152 | tf_op jit(solution)/shard_map/all_to_all | solution.py:92
  294.1 15.6 %copy-start.1 = (bf16[32,1024]{1,0:T(8,128)(2,1)S(1)}, bf16[32,1024]{1,0:T(8,128)(2,1)}, u32[]{:S(2)}) copy-start(bf16[32,1024]{1,0:T(8,128)(2,1)} %param.7) | copy-start | bytes 196612
Sparse Core Ops, SparseCore 0:
  75.9 88.3 all-reduce.2
  167.2 31.1 reduce-scatter.3
  205.6 39.3 all-gather.1
